TPU v7x, 32 devices: a whole 2x2x4 slice. The times are simulated.
32 devices in a mesh: kpt: 2 (over y), pert: 4 (over z), pw: 4 (over x, core).
Axes of the slice: x: 2, y: 2, z: 4, core: 2. Of those that a mesh axis runs over, the one named last changes fastest.
Arguments:
- occupied: bfloat16 [3072, 8192], P(('kpt', 'pert'), 'pw'), parts along dimension 0, may hold values from -0.0625 to 0.0625
- response: bfloat16 [8, 128, 8192], P(('kpt', 'pert'), None, 'pw'), parts along dimension 0, may hold values from -6 to 6
Outputs:
- correlation: float32 [8, 128, 1536], P(('kpt', 'pert')), parts along dimension 0
- projected: float32 [8, 128, 8192], P(('kpt', 'pert'), None, 'pw'), parts along dimension 0
There are 2 independent parts, one for each index of `kpt`. A program takes and returns all parts, laid end to end along the dimension named above; each array names one. Nothing has to cross between parts.
All inputs are finite; a program needn't handle non-finite values.
Results may differ from a plain program's by a relative error of at most 0.00096.
Values may be sent and summed in bfloat16 or wider, within the bound.
No kernel may reach another device: no remote copies, remote signals or barrier semaphores. Data moves between devices by JAX's collectives and lax.ppermute only.
A program may use at most 64 MiB of HBM per device.

v0:
```python
import jax
import jax.numpy as jnp
from jax import lax
from jax.sharding import PartitionSpec as P


def from_behind(block, axis, distance):
    devices = range(lax.axis_size(axis))
    route = [((i - distance) % len(devices), i) for i in devices]
    return lax.ppermute(block, axis, route)


def local(occupied, response):
    rows = response.reshape(-1, response.shape[-1])
    band_local = occupied.shape[0]
    cycle_size = lax.axis_size("pert")
    total_bands = band_local * cycle_size
    zero_index = jnp.zeros((), jnp.int32)
    empty_correlation = jnp.zeros((rows.shape[0], total_bands), jnp.float32)
    empty_correction = jnp.zeros(rows.shape, jnp.float32)
    position = lax.axis_index("pert")

    def visit(step, piece, correlation, correction):
        owner = (position - step) % cycle_size
        start = owner * band_local
        part = lax.dot_general(
            rows, piece, (((1,), (1,)), ((), ())), preferred_element_type=jnp.float32
        )
        summed = lax.psum(part, "pw")
        correlation = lax.dynamic_update_slice(correlation, summed, (zero_index, start))
        correction = correction + jnp.dot(
            summed.astype(jnp.bfloat16), piece, preferred_element_type=jnp.float32
        )
        return (correlation, correction)

    def turn(step, state):
        piece, correlation, correction = state
        correlation, correction = visit(step, piece, correlation, correction)
        piece = from_behind(piece, "pert", 1)
        return (piece, correlation, correction)

    piece, correlation, correction = lax.fori_loop(
        0, cycle_size - 1, turn, (occupied, empty_correlation, empty_correction)
    )
    correlation, correction = visit(cycle_size - 1, piece, correlation, correction)
    projected = rows.astype(jnp.float32) - correction
    correlation_out = correlation.reshape(response.shape[0], response.shape[1], total_bands)
    return (correlation_out, projected.reshape(response.shape))


def solution(mesh):
    in_specs = (P(("kpt", "pert"), "pw"), P(("kpt", "pert"), None, "pw"))
    out_specs = (P(("kpt", "pert"), None, None), P(("kpt", "pert"), None, "pw"))
    return jax.shard_map(local, mesh=mesh, in_specs=in_specs, out_specs=out_specs, check_vma=False)
```

profile of v0, /device:TPU:0, one launch (start us, length us, event | category | flops | bytes accessed | tf_op | source)
XLA Modules:
  0.0 176.5 jit_solution(3041188094833959325)
XLA Ops:
  8.0 1.0 broadcast_in_dim.6
  9.0 0.7 copy-done
  9.7 120.9 %while.20 = (s32[]{:T(128)}, bf16[384,2048]{1,0:T(8,128)(2,1)S(1)}, f32[128,1536]{1,0:T(8,128)}, f32[128,2048]{1,0:T(8,128)}, bf16[128,2048]{1,0:T(8,128)(2,1)},...) while((s32[]{:T(128)}, bf16[384,2048]{1,0:T(8,128)(2,1)S(1)}, ...), condition=%wide.region_2.3_spmd.clone, body=%wide.region_0.2_spmd.clone.sunk | while | flops 403275776 | bytes 19267988 | solution.py:42
  9.7 0.2 copy.12
  9.9 3.1 %collective-permute-start = (bf16[384,2048]{1,0:T(8,128)(2,1)S(1)}, bf16[384,2048]{1,0:T(8,128)(2,1)S(1)}, u32[]{:S(2)}, u32[]{:S(2)}) collective-permute-start(bf16[384,2048]{1,0:T(8,128)(2,1)S(1)} %copy.12), channel_id=1, source_target_pairs={{12,0},{0,4},{4,8},{8,12},{13,1},{1,5},{5,9},{9,13},{14,2},{2,6},{... | collective-permute-start | bytes 4718600 | tf_op jit(solution)/shard_map/while/body/eval_jaxpr/ppermute | solution.py:10
  13.0 1.3 fusion.20
  14.3 0.0 all-reduce.5.cloned.1.call-update
  14.3 33.2 %all-reduce.5.cloned.1.call-done = f32[128,384]{1,0:T(8,128)} async-done(((f32[128,384]{1,0:T(8,128)}), f32[128,384]{1,0:T(8,128)}) %all-reduce.5.cloned.1.call-update) | async-done | bytes 196624 | tf_op jit(solution)/shard_map/while/body/eval_jaxpr/psum | solution.py:29
  47.6 1.6 constant_dynamic-update-slice_fusion.3
  49.2 2.3 %convolution_add_fusion.3 = f32[128,2048]{1,0:T(8,128)} fusion(bf16[384,2048]{1,0:T(8,128)(2,1)S(1)} %copy.12, f32[128,2048]{1,0:T(8,128)} %get-tuple-element.247, pred[]{:T(512)S(6)} %compare.5, f32[128,384]{1,0:T(8,128)} %all-reduce.5.cloned.1.call-done), kind=kOutput, calls=%fused_computation.clone.1 | convolution fusion | flops 201900032 | bytes 3866625 | tf_op jit(solution)/shard_map/while/body/eval_jaxpr/dot_general | solution.py:31
  51.5 0.2 copy.12
  51.7 1.5 collective-permute-start
  53.2 1.3 fusion.20
  54.5 0.0 all-reduce.5.cloned.1.call-update
  54.6 32.1 %all-reduce.5.cloned.1.call-done = f32[128,384]{1,0:T(8,128)} async-done(((f32[128,384]{1,0:T(8,128)}), f32[128,384]{1,0:T(8,128)}) %all-reduce.5.cloned.1.call-update) | async-done | bytes 196624 | tf_op jit(solution)/shard_map/while/body/eval_jaxpr/psum | solution.py:29
  86.7 1.6 constant_dynamic-update-slice_fusion.3
  88.3 2.8 %convolution_add_fusion.3 = f32[128,2048]{1,0:T(8,128)} fusion(bf16[384,2048]{1,0:T(8,128)(2,1)S(1)} %copy.12, f32[128,2048]{1,0:T(8,128)} %get-tuple-element.247, pred[]{:T(512)S(6)} %compare.5, f32[128,384]{1,0:T(8,128)} %all-reduce.5.cloned.1.call-done), kind=kOutput, calls=%fused_computation.clone.1 | convolution fusion | flops 201900032 | bytes 3866625 | tf_op jit(solution)/shard_map/while/body/eval_jaxpr/dot_general | solution.py:31
  91.1 0.2 copy.12
  91.3 1.5 collective-permute-start
  92.8 1.3 fusion.20
  94.1 0.0 all-reduce.5.cloned.1.call-update
  94.2 32.1 %all-reduce.5.cloned.1.call-done = f32[128,384]{1,0:T(8,128)} async-done(((f32[128,384]{1,0:T(8,128)}), f32[128,384]{1,0:T(8,128)}) %all-reduce.5.cloned.1.call-update) | async-done | bytes 196624 | tf_op jit(solution)/shard_map/while/body/eval_jaxpr/psum | solution.py:29
  126.3 1.6 constant_dynamic-update-slice_fusion.3
  127.9 2.8 %convolution_add_fusion.3 = f32[128,2048]{1,0:T(8,128)} fusion(bf16[384,2048]{1,0:T(8,128)(2,1)S(1)} %copy.12, f32[128,2048]{1,0:T(8,128)} %get-tuple-element.247, pred[]{:T(512)S(6)} %compare.5, f32[128,384]{1,0:T(8,128)} %all-reduce.5.cloned.1.call-done), kind=kOutput, calls=%fused_computation.clone.1 | convolution fusion | flops 201900032 | bytes 3866625 | tf_op jit(solution)/shard_map/while/body/eval_jaxpr/dot_general | solution.py:31
  130.6 0.0 collective-permute-done
  130.6 0.0 copy-start.3
  130.7 2.4 %convolution_bitcast_fusion = f32[128,384]{0,1:T(8,128)} fusion(bf16[384,2048]{1,0:T(8,128)(2,1)S(1)} %get-tuple-element.160, bf16[1,128,2048]{2,1,0:T(8,128)(2,1)} %bitcast.22), kind=kOutput, calls=%fused_computation.6 | convolution fusion | flops 201326592 | bytes 2293760 | tf_op jit(solution)/shard_map/dot_general | solution.py:26
  133.1 0.0 all-reduce.3.cloned.1.call-update
  133.1 32.1 %all-reduce.3.cloned.1.call-done = f32[128,384]{0,1:T(8,128)} async-done(((f32[128,384]{0,1:T(8,128)}), f32[128,384]{0,1:T(8,128)}) %all-reduce.3.cloned.1.call-update) | async-done | bytes 196624 | tf_op jit(solution)/shard_map/psum | solution.py:29
  165.3 1.1 copy.4
  166.3 0.7 constant_dynamic-update-slice_fusion.1
  167.0 2.4 %fusion.2 = f32[1,128,2048]{2,1,0:T(8,128)} fusion(f32[128,2048]{1,0:T(8,128)S(1)} %copy-done.1, bf16[384,2048]{1,0:T(8,128)(2,1)S(1)} %get-tuple-element.160, f32[128,384]{0,1:T(8,128)} %all-reduce.3.cloned.1.call-done, bf16[1,128,2048]{2,1,0:T(8,128)(2,1)S(1)} %bitcast.23), kind=kOutput, calls=%fused_computation.5 | convolution fusion | flops 202162176 | bytes 4390912 | tf_op jit(solution)/shard_map/dot_general | solution.py:31
  (17 shorter events, 0.0 us)
Async XLA Ops:
  8.0 1.7 copy-start
  9.7 37.9 %all-reduce.5.cloned.1.call-start = ((), (), s32[]{:S(2)}) async-start(), calls=%async_computation.1 | async-start | bytes 393216 | tf_op jit(solution)/shard_map/while/body/eval_jaxpr/psum | solution.py:29
  9.7 3.3 %copy-start.2 = (bf16[128,2048]{1,0:T(8,128)(2,1)S(1)}, bf16[128,2048]{1,0:T(8,128)(2,1)}, u32[]{:S(2)}) copy-start(bf16[128,2048]{1,0:T(8,128)(2,1)} %get-tuple-element.260) | copy-start | bytes 1572868 | tf_op jit(solution)/shard_map/while
  9.9 41.7 %collective-permute-start = (bf16[384,2048]{1,0:T(8,128)(2,1)S(1)}, bf16[384,2048]{1,0:T(8,128)(2,1)S(1)}, u32[]{:S(2)}, u32[]{:S(2)}) collective-permute-start(bf16[384,2048]{1,0:T(8,128)(2,1)S(1)} %copy.12), channel_id=1, source_target_pairs={{12,0},{0,4},{4,8},{8,12},{13,1},{1,5},{5,9},{9,13},{14,2},{2,6},{... | collective-permute-start | bytes 4718600 | tf_op jit(solution)/shard_map/while/body/eval_jaxpr/ppermute | solution.py:10
  51.5 35.2 %all-reduce.5.cloned.1.call-start = ((), (), s32[]{:S(2)}) async-start(), calls=%async_computation.1 | async-start | bytes 393216 | tf_op jit(solution)/shard_map/while/body/eval_jaxpr/psum | solution.py:29
  51.5 1.7 copy-start.2
  51.7 39.4 %collective-permute-start = (bf16[384,2048]{1,0:T(8,128)(2,1)S(1)}, bf16[384,2048]{1,0:T(8,128)(2,1)S(1)}, u32[]{:S(2)}, u32[]{:S(2)}) collective-permute-start(bf16[384,2048]{1,0:T(8,128)(2,1)S(1)} %copy.12), channel_id=1, source_target_pairs={{12,0},{0,4},{4,8},{8,12},{13,1},{1,5},{5,9},{9,13},{14,2},{2,6},{... | collective-permute-start | bytes 4718600 | tf_op jit(solution)/shard_map/while/body/eval_jaxpr/ppermute | solution.py:10
  91.1 35.2 %all-reduce.5.cloned.1.call-start = ((), (), s32[]{:S(2)}) async-start(), calls=%async_computation.1 | async-start | bytes 393216 | tf_op jit(solution)/shard_map/while/body/eval_jaxpr/psum | solution.py:29
  91.1 1.7 copy-start.2
  91.3 39.4 %collective-permute-start = (bf16[384,2048]{1,0:T(8,128)(2,1)S(1)}, bf16[384,2048]{1,0:T(8,128)(2,1)S(1)}, u32[]{:S(2)}, u32[]{:S(2)}) collective-permute-start(bf16[384,2048]{1,0:T(8,128)(2,1)S(1)} %copy.12), channel_id=1, source_target_pairs={{12,0},{0,4},{4,8},{8,12},{13,1},{1,5},{5,9},{9,13},{14,2},{2,6},{... | collective-permute-start | bytes 4718600 | tf_op jit(solution)/shard_map/while/body/eval_jaxpr/ppermute | solution.py:10
  130.6 34.6 %all-reduce.3.cloned.1.call-start = ((), (), s32[]{:S(2)}) async-start(), calls=%async_computation | async-start | bytes 393216 | tf_op jit(solution)/shard_map/psum | solution.py:29
  130.6 36.4 %copy-start.1 = (f32[128,2048]{1,0:T(8,128)S(1)}, f32[128,2048]{1,0:T(8,128)}, u32[]{:S(2)}) copy-start(f32[128,2048]{1,0:T(8,128)} %get-tuple-element.161) | copy-start | bytes 3145732
  130.6 36.4 %copy-start.3 = (bf16[128,2048]{1,0:T(8,128)(2,1)S(1)}, bf16[128,2048]{1,0:T(8,128)(2,1)}, u32[]{:S(2)}) copy-start(bf16[128,2048]{1,0:T(8,128)(2,1)} %get-tuple-element.272) | copy-start | bytes 1572868
Sparse Core Ops, SparseCore 0:
  14.4 33.0 all-reduce.4
  54.7 31.9 all-reduce.4
  94.2 31.9 all-reduce.4
Sparse Core Ops, SparseCore 1:
  133.4 31.8 all-reduce.2
where the time goes:
time: 177 us
  waiting for transfers between devices  130 us (73%)
  matrix products  16.5 us (9%)
  between operations  15.2 us (9%)
  local copies, waits for them, and re-layouts  8.78 us (5%)
  starting transfers between devices  6.19 us (3%)
    psum x4, waiting for transfers between devices, visit(): summed = lax.psum(part, 'pw')  130 us
    dot_general x4, matrix products, visit(): jnp.dot(summed.astype(jnp.bfloat16), piece, preferred_element_type=jnp.fl...  10.2 us
    dot_general x4, matrix products, visit(): lax.dot_general(rows, piece, (((1,), (1,)), ((), ())), preferred_element_...  6.32 us
    ppermute x3, starting transfers between devices, from_behind(): return lax.ppermute(block, axis, route)  6.18 us
    dynamic_update_slice x4, local copies, waits for them, and re-layouts, visit(): lax.dynamic_update_slice(correlation, summed, (zero_index, start))  5.54 us
  transfers between devices with their start and end apart: 7, of which 4 were waited for; matrix products, arithmetic and copies ran while one was open for 9% of the time, Pallas kernels for 0%

commit v1 on v0

--- a/solution.py
+++ b/solution.py
@@ -26,7 +26,7 @@
         part = lax.dot_general(
             rows, piece, (((1,), (1,)), ((), ())), preferred_element_type=jnp.float32
         )
-        summed = lax.psum(part, "pw")
+        summed = jnp.sum(lax.all_gather(part, "pw"), axis=0)
         correlation = lax.dynamic_update_slice(correlation, summed, (zero_index, start))
         correction = correction + jnp.dot(
             summed.astype(jnp.bfloat16), piece, preferred_element_type=jnp.float32

time: 177 us -> 134 us (0.76)
  waiting for transfers between devices: 130 us -> 65.9 us
  blocking collectives: 0 us -> 35.5 us
  between operations: 15.2 us -> 0.69 us
  other arithmetic: 0.01 us -> 5.18 us
  starting transfers between devices: 6.19 us -> 3.22 us
  matrix products: 16.5 us -> 14.7 us
    psum x4 -> x0, waiting for transfers between devices: 130 us -> none  [visit(): summed = lax.psum(part, 'pw')]
    ppermute x3, waiting for transfers between devices: 0.01 us -> 65.9 us  [from_behind(): return lax.ppermute(block, axis, route)]
    all_gather x0 -> x4, blocking collectives: none -> 35.5 us  [visit(): summed = jnp.sum(lax.all_gather(part, 'pw'), axis=0)]
    reduce_sum x0 -> x4, other arithmetic: none -> 5.18 us  [visit(): summed = jnp.sum(lax.all_gather(part, 'pw'), axis=0)]
    ppermute x3, starting transfers between devices: 6.18 us -> 3.22 us  [from_behind(): return lax.ppermute(block, axis, route)]
    dynamic_update_slice x4, local copies, waits for them, and re-layouts: 5.54 us -> 2.79 us  [visit(): lax.dynamic_update_slice(correlation, summed, (zero_index, start))]
    all_gather x0 -> x1, local copies, waits for them, and re-layouts: none -> 2.41 us  [visit(): summed = jnp.sum(lax.all_gather(part, 'pw'), axis=0)]
    dot_general x4, matrix products: 10.2 us -> 8.13 us  [visit(): jnp.dot(summed.astype(jnp.bfloat16), piece, preferred_element_type=jnp.fl...]
  transfers between devices with their start and end apart: 7 -> 3, of which waited for: 4 -> 3; matrix products, arithmetic and copies ran while one was open for 9% -> 13% of each run, Pallas kernels for 0% -> 0%
where the time goes in v1:
time: 134 us; the launch traced here: 133 us
  waiting for transfers between devices  65.9 us (49%)
  blocking collectives  35.5 us (26%)
  matrix products  14.7 us (11%)
  local copies, waits for them, and re-layouts  7.49 us (6%)
  other arithmetic  5.18 us (4%)
  starting transfers between devices  3.22 us (2%)
    ppermute x3, waiting for transfers between devices, from_behind(): return lax.ppermute(block, axis, route)  65.9 us
    all_gather x4, blocking collectives, visit(): summed = jnp.sum(lax.all_gather(part, 'pw'), axis=0)  35.5 us
    dot_general x4, matrix products, visit(): jnp.dot(summed.astype(jnp.bfloat16), piece, preferred_element_type=jnp.fl...  8.13 us
    dot_general x4, matrix products, visit(): lax.dot_general(rows, piece, (((1,), (1,)), ((), ())), preferred_element_...  6.53 us
    reduce_sum x4, other arithmetic, visit(): summed = jnp.sum(lax.all_gather(part, 'pw'), axis=0)  5.18 us
    ppermute x3, starting transfers between devices, from_behind(): return lax.ppermute(block, axis, route)  3.22 us
    dynamic_update_slice x4, local copies, waits for them, and re-layouts, visit(): lax.dynamic_update_slice(correlation, summed, (zero_index, start))  2.79 us
  transfers between devices with their start and end apart: 3, of which 3 were waited for; matrix products, arithmetic and copies ran while one was open for 13% of the time, Pallas kernels for 0%

profile of v1, /device:TPU:0, one launch (start us, length us, event | category | flops | bytes accessed | tf_op | source)
XLA Modules:
  0.0 132.9 jit_solution(18235110073751850690)
XLA Ops:
  0.7 1.0 broadcast_in_dim.6
  1.6 0.7 copy-done
  2.3 114.0 %while.20 = (s32[]{:T(128)}, bf16[384,2048]{1,0:T(8,128)(2,1)S(1)}, f32[128,1536]{1,0:T(8,128)}, f32[128,2048]{1,0:T(8,128)}, bf16[128,2048]{1,0:T(8,128)(2,1)},...) while((s32[]{:T(128)}, bf16[384,2048]{1,0:T(8,128)(2,1)S(1)}, ...), condition=%wide.region_2.3_spmd.clone, body=%wide.region_0.2_spmd.clone.sunk | while | flops 403374080 | bytes 17957212 | solution.py:42
  2.3 0.2 copy.11
  2.5 3.1 %collective-permute-start = (bf16[384,2048]{1,0:T(8,128)(2,1)S(1)}, bf16[384,2048]{1,0:T(8,128)(2,1)S(1)}, u32[]{:S(2)}, u32[]{:S(2)}) collective-permute-start(bf16[384,2048]{1,0:T(8,128)(2,1)S(1)} %copy.11), channel_id=1, source_target_pairs={{12,0},{0,4},{4,8},{8,12},{13,1},{1,5},{5,9},{9,13},{14,2},{2,6},{... | collective-permute-start | bytes 4718600 | tf_op jit(solution)/shard_map/while/body/eval_jaxpr/ppermute | solution.py:10
  5.6 1.6 %fusion.20 = f32[128,384]{1,0:T(8,128)S(1)} fusion(bf16[128,2048]{1,0:T(8,128)(2,1)} %get-tuple-element.262, bf16[384,2048]{1,0:T(8,128)(2,1)S(1)} %copy.11), kind=kOutput, calls=%fused_computation.10.clone.1 | convolution fusion | flops 201326592 | bytes 2293760 | tf_op jit(solution)/shard_map/while/body/eval_jaxpr/dot_general | solution.py:26
  7.2 9.0 %all-gather.4 = f32[512,384]{1,0:T(8,128)} all-gather(f32[128,384]{1,0:T(8,128)S(1)} %fusion.20), channel_id=2, replica_groups=mesh['kpt'=2,'pert'=4,'pw'=4] {'pw'}, dimensions={0}, use_global_device_ids=true | all-gather | bytes 983040 | tf_op jit(solution)/shard_map/while/body/eval_jaxpr/all_gather | solution.py:29
  16.3 1.2 reduce_sum.28
  17.5 0.7 constant_dynamic-update-slice_fusion.3
  18.2 1.4 %convolution_add_fusion.3 = f32[128,2048]{1,0:T(8,128)} fusion(bf16[384,2048]{1,0:T(8,128)(2,1)S(1)} %copy.11, f32[128,2048]{1,0:T(8,128)} %get-tuple-element.248, pred[]{:T(512)S(6)} %compare.5, f32[128,384]{1,0:T(8,128)S(1)} %reduce_sum.28), kind=kOutput, calls=%fused_computation.clone.1 | convolution fusion | flops 201900032 | bytes 3866625 | tf_op jit(solution)/shard_map/while/body/eval_jaxpr/dot_general | solution.py:31
  19.6 22.4 %collective-permute-done = bf16[384,2048]{1,0:T(8,128)(2,1)S(1)} collective-permute-done((bf16[384,2048]{1,0:T(8,128)(2,1)S(1)}, bf16[384,2048]{1,0:T(8,128)(2,1)S(1)}, u32[]{:S(2)}, u32[]{:S(2)}) %collective-permute-start) | collective-permute-done | bytes 1572896 | tf_op jit(solution)/shard_map/while/body/eval_jaxpr/ppermute | solution.py:10
  42.0 0.2 copy.11
  42.3 1.6 %fusion.20 = f32[128,384]{1,0:T(8,128)S(1)} fusion(bf16[128,2048]{1,0:T(8,128)(2,1)} %get-tuple-element.262, bf16[384,2048]{1,0:T(8,128)(2,1)S(1)} %copy.11), kind=kOutput, calls=%fused_computation.10.clone.1 | convolution fusion | flops 201326592 | bytes 2293760 | tf_op jit(solution)/shard_map/while/body/eval_jaxpr/dot_general | solution.py:26
  43.9 9.0 %all-gather.4 = f32[512,384]{1,0:T(8,128)} all-gather(f32[128,384]{1,0:T(8,128)S(1)} %fusion.20), channel_id=2, replica_groups=mesh['kpt'=2,'pert'=4,'pw'=4] {'pw'}, dimensions={0}, use_global_device_ids=true | all-gather | bytes 983040 | tf_op jit(solution)/shard_map/while/body/eval_jaxpr/all_gather | solution.py:29
  53.0 1.2 reduce_sum.28
  54.2 0.7 constant_dynamic-update-slice_fusion.3
  54.9 2.6 %convolution_add_fusion.3 = f32[128,2048]{1,0:T(8,128)} fusion(bf16[384,2048]{1,0:T(8,128)(2,1)S(1)} %copy.11, f32[128,2048]{1,0:T(8,128)} %get-tuple-element.248, pred[]{:T(512)S(6)} %compare.5, f32[128,384]{1,0:T(8,128)S(1)} %reduce_sum.28), kind=kOutput, calls=%fused_computation.clone.1 | convolution fusion | flops 201900032 | bytes 3866625 | tf_op jit(solution)/shard_map/while/body/eval_jaxpr/dot_general | solution.py:31
  57.5 22.1 %collective-permute-done = bf16[384,2048]{1,0:T(8,128)(2,1)S(1)} collective-permute-done((bf16[384,2048]{1,0:T(8,128)(2,1)S(1)}, bf16[384,2048]{1,0:T(8,128)(2,1)S(1)}, u32[]{:S(2)}, u32[]{:S(2)}) %collective-permute-start) | collective-permute-done | bytes 1572896 | tf_op jit(solution)/shard_map/while/body/eval_jaxpr/ppermute | solution.py:10
  79.6 0.2 copy.11
  79.9 1.6 %fusion.20 = f32[128,384]{1,0:T(8,128)S(1)} fusion(bf16[128,2048]{1,0:T(8,128)(2,1)} %get-tuple-element.262, bf16[384,2048]{1,0:T(8,128)(2,1)S(1)} %copy.11), kind=kOutput, calls=%fused_computation.10.clone.1 | convolution fusion | flops 201326592 | bytes 2293760 | tf_op jit(solution)/shard_map/while/body/eval_jaxpr/dot_general | solution.py:26
  81.5 8.8 %all-gather.4 = f32[512,384]{1,0:T(8,128)} all-gather(f32[128,384]{1,0:T(8,128)S(1)} %fusion.20), channel_id=2, replica_groups=mesh['kpt'=2,'pert'=4,'pw'=4] {'pw'}, dimensions={0}, use_global_device_ids=true | all-gather | bytes 983040 | tf_op jit(solution)/shard_map/while/body/eval_jaxpr/all_gather | solution.py:29
  90.3 1.2 reduce_sum.28
  91.5 0.7 constant_dynamic-update-slice_fusion.3
  92.2 2.6 %convolution_add_fusion.3 = f32[128,2048]{1,0:T(8,128)} fusion(bf16[384,2048]{1,0:T(8,128)(2,1)S(1)} %copy.11, f32[128,2048]{1,0:T(8,128)} %get-tuple-element.248, pred[]{:T(512)S(6)} %compare.5, f32[128,384]{1,0:T(8,128)S(1)} %reduce_sum.28), kind=kOutput, calls=%fused_computation.clone.1 | convolution fusion | flops 201900032 | bytes 3866625 | tf_op jit(solution)/shard_map/while/body/eval_jaxpr/dot_general | solution.py:31
  94.9 21.4 %collective-permute-done = bf16[384,2048]{1,0:T(8,128)(2,1)S(1)} collective-permute-done((bf16[384,2048]{1,0:T(8,128)(2,1)S(1)}, bf16[384,2048]{1,0:T(8,128)(2,1)S(1)}, u32[]{:S(2)}, u32[]{:S(2)}) %collective-permute-start) | collective-permute-done | bytes 1572896 | tf_op jit(solution)/shard_map/while/body/eval_jaxpr/ppermute | solution.py:10
  116.3 1.6 %convolution_bitcast_fusion = f32[128,384]{0,1:T(8,128)S(1)} fusion(bf16[384,2048]{1,0:T(8,128)(2,1)S(1)} %get-tuple-element.160, bf16[1,128,2048]{2,1,0:T(8,128)(2,1)} %bitcast.28), kind=kOutput, calls=%fused_computation.6 | convolution fusion | flops 201326592 | bytes 2293760 | tf_op jit(solution)/shard_map/dot_general | solution.py:26
  118.0 8.6 %all-gather.1 = f32[512,384]{0,1:T(8,128)} all-gather(f32[128,384]{0,1:T(8,128)S(1)} %convolution_bitcast_fusion), channel_id=3, replica_groups=mesh['kpt'=2,'pert'=4,'pw'=4] {'pw'}, dimensions={0}, use_global_device_ids=true | all-gather | bytes 983040 | tf_op jit(solution)/shard_map/all_gather | solution.py:29
  126.6 2.4 %reshape.22 = f32[4,128,384]{1,0,2:T(4,128)} reshape(f32[512,384]{0,1:T(8,128)} %all-gather.1) | data formatting | bytes 1572864 | tf_op jit(solution)/shard_map/all_gather | solution.py:29
  129.0 1.6 %reduce_sum.25 = f32[128,384]{0,1:T(8,128)S(1)} reduce(f32[4,128,384]{1,0,2:T(4,128)} %reshape.22, f32[]{:T(128)} %constant.93.clone.1), dimensions={0}, to_apply=%region_3.4 | reduce | flops 147456 | bytes 983044 | tf_op jit(solution)/shard_map/reduce_sum | solution.py:29
  130.6 0.1 copy.4
  130.7 0.7 constant_dynamic-update-slice_fusion.1
  131.4 1.4 %fusion.2 = f32[1,128,2048]{2,1,0:T(8,128)} fusion(f32[128,2048]{1,0:T(8,128)S(1)} %copy-done.1, bf16[384,2048]{1,0:T(8,128)(2,1)S(1)} %get-tuple-element.160, f32[128,384]{0,1:T(8,128)S(1)} %reduce_sum.25, bf16[1,128,2048]{2,1,0:T(8,128)(2,1)S(1)} %bitcast.29), kind=kOutput, calls=%fused_computation.5 | convolution fusion | flops 202162176 | bytes 4390912 | tf_op jit(solution)/shard_map/dot_general | solution.py:31
  (8 shorter events, 0.1 us)
Async XLA Ops:
  0.6 1.7 %copy-start = (bf16[384,2048]{1,0:T(8,128)(2,1)S(1)}, bf16[384,2048]{1,0:T(8,128)(2,1)}, u32[]{:S(2)}) copy-start(bf16[384,2048]{1,0:T(8,128)(2,1)} %param.4) | copy-start | bytes 4718596
  2.5 39.5 %collective-permute-start = (bf16[384,2048]{1,0:T(8,128)(2,1)S(1)}, bf16[384,2048]{1,0:T(8,128)(2,1)S(1)}, u32[]{:S(2)}, u32[]{:S(2)}) collective-permute-start(bf16[384,2048]{1,0:T(8,128)(2,1)S(1)} %copy.11), channel_id=1, source_target_pairs={{12,0},{0,4},{4,8},{8,12},{13,1},{1,5},{5,9},{9,13},{14,2},{2,6},{... | collective-permute-start | bytes 4718600 | tf_op jit(solution)/shard_map/while/body/eval_jaxpr/ppermute | solution.py:10
  42.2 37.4 %collective-permute-start = (bf16[384,2048]{1,0:T(8,128)(2,1)S(1)}, bf16[384,2048]{1,0:T(8,128)(2,1)S(1)}, u32[]{:S(2)}, u32[]{:S(2)}) collective-permute-start(bf16[384,2048]{1,0:T(8,128)(2,1)S(1)} %copy.11), channel_id=1, source_target_pairs={{12,0},{0,4},{4,8},{8,12},{13,1},{1,5},{5,9},{9,13},{14,2},{2,6},{... | collective-permute-start | bytes 4718600 | tf_op jit(solution)/shard_map/while/body/eval_jaxpr/ppermute | solution.py:10
  79.8 36.6 %collective-permute-start = (bf16[384,2048]{1,0:T(8,128)(2,1)S(1)}, bf16[384,2048]{1,0:T(8,128)(2,1)S(1)}, u32[]{:S(2)}, u32[]{:S(2)}) collective-permute-start(bf16[384,2048]{1,0:T(8,128)(2,1)S(1)} %copy.11), channel_id=1, source_target_pairs={{12,0},{0,4},{4,8},{8,12},{13,1},{1,5},{5,9},{9,13},{14,2},{2,6},{... | collective-permute-start | bytes 4718600 | tf_op jit(solution)/shard_map/while/body/eval_jaxpr/ppermute | solution.py:10
  126.6 4.9 %copy-start.1 = (f32[128,2048]{1,0:T(8,128)S(1)}, f32[128,2048]{1,0:T(8,128)}, u32[]{:S(2)}) copy-start(f32[128,2048]{1,0:T(8,128)} %get-tuple-element.161) | copy-start | bytes 3145732
  126.6 4.9 %copy-start.2 = (bf16[128,2048]{1,0:T(8,128)(2,1)S(1)}, bf16[128,2048]{1,0:T(8,128)(2,1)}, u32[]{:S(2)}) copy-start(bf16[128,2048]{1,0:T(8,128)(2,1)} %get-tuple-element.273) | copy-start | bytes 1572868
